TPU v7x, 32 devices: a whole 2x2x4 slice. The times are simulated.
32 devices in a mesh: dp: 8 (over y, x, core), mp: 4 (over z).
Axes of the slice: x: 2, y: 2, z: 4, core: 2. Of those that a mesh axis runs over, the one named last changes fastest.
Arguments:
- caption_tokens: bfloat16 [784, 16, 768], P('dp'), may hold values from -6 to 6
- image_tokens: bfloat16 [224, 50, 768], P(('dp', 'mp')), may hold values from -6 to 6
- image_attend: bfloat16 [3, 768, 768], replicated, may hold values from -0.21875 to 0.21875
- image_output: bfloat16 [768, 768], replicated, may hold values from -0.4375 to 0.4375
- image_expand: bfloat16 [768, 3072], replicated, may hold values from -0.21875 to 0.21875
- image_reduce: bfloat16 [3072, 768], replicated, may hold values from -0.109375 to 0.109375
- image_gains: float32 [2, 768], replicated, may hold values from 0.1 to 1.9
- caption_attend: bfloat16 [3, 768, 768], P(None, None, 'mp'), may hold values from -0.21875 to 0.21875
- attend_bias: float32 [2, 768], P(None, 'mp'), may hold values from -3 to 3
- caption_output: bfloat16 [768, 768], P('mp'), may hold values from -0.4375 to 0.4375
- output_bias: float32 [768], replicated, may hold values from -1 to 1
- caption_expand: bfloat16 [768, 3072], P(None, 'mp'), may hold values from -0.21875 to 0.21875
- expand_bias: float32 [3072], P('mp'), may hold values from -3 to 3
- caption_reduce: bfloat16 [3072, 768], P('mp'), may hold values from -0.109375 to 0.109375
- reduce_bias: float32 [768], replicated, may hold values from -1 to 1
- norm_gains: float32 [2, 768], replicated, may hold values from 0.1 to 1.9
- norm_shifts: float32 [2, 768], replicated, may hold values from -2 to 2
- log_scale: float32 [1], replicated, may hold values from 3.6 to 4.4
- caption_image: int32 [784], P('dp'), may hold values from 0 to 223, as said below
Outputs:
- contrast_loss: float32 [1], replicated
- gradient_tokens: float32 [784, 16, 768], P('dp')
- gradient_attend: float32 [3, 768, 768], P(None, None, 'mp')
- gradient_attend_bias: float32 [2, 768], P(None, 'mp')
- gradient_output: float32 [768, 768], P('mp')
- gradient_output_bias: float32 [768], replicated
- gradient_expand: float32 [768, 3072], P(None, 'mp')
- gradient_expand_bias: float32 [3072], P('mp')
- gradient_reduce: float32 [3072, 768], P('mp')
- gradient_reduce_bias: float32 [768], replicated
- gradient_gains: float32 [2, 768], replicated
- gradient_shifts: float32 [2, 768], replicated
- gradient_log_scale: float32 [1], replicated
Inputs may be any that keep to these rules, and one draw needn't show every extreme that they name: `caption_image`: every image is named by at least one and at most five captions.
All inputs are finite; a program needn't handle non-finite values.
Results may differ from a plain program's by a relative error of at most 0.014.
Values may be sent and summed in bfloat16 or wider, within the bound.
A program may use at most 128 MiB of HBM per device.

v0:
```python
from functools import partial
import jax
import jax.numpy as jnp
from jax import lax
from jax.sharding import PartitionSpec as P

HEAD_DIM = 64


def norm_rows(values, gains, shifts):
    centred = values - jnp.mean(values, axis=-1, keepdims=True)
    variance = jnp.mean(centred * centred, axis=-1, keepdims=True)
    return centred * lax.rsqrt(variance + 1e-06) * gains + shifts


def softmax_last(logits):
    highest = jnp.max(logits, axis=-1, keepdims=True)
    expos = jnp.exp(logits - highest)
    return expos / jnp.sum(expos, axis=-1, keepdims=True)


def unit_rows(pooled):
    return pooled * lax.rsqrt(jnp.sum(pooled * pooled, axis=-1, keepdims=True) + 1e-06)


def matmul(left_side, right_side):
    return jnp.dot(left_side, right_side, preferred_element_type=jnp.float32)


def contract_last(left_side, right_side):
    return lax.dot_general(
        left_side, right_side, (((1,), (1,)), ((), ())), preferred_element_type=jnp.float32
    )


def outer_sum(left_side, right_side):
    return lax.dot_general(
        left_side, right_side, (((0,), (0,)), ((), ())), preferred_element_type=jnp.float32
    )


def contract(formula, left_side, right_side):
    return jnp.einsum(formula, left_side, right_side, preferred_element_type=jnp.float32)


def image_block(tokens, image_attend, image_output, image_expand, image_reduce, image_gains):
    group_size, length, model_width = tokens.shape
    heads_count = model_width // HEAD_DIM
    heads_shape = (group_size, length, heads_count, HEAD_DIM)
    flattened = tokens.astype(jnp.float32).reshape(group_size * length, model_width)
    normed = norm_rows(flattened, image_gains[0], 0.0).astype(jnp.bfloat16)
    queries = matmul(normed, image_attend[0]).astype(jnp.bfloat16).reshape(heads_shape)
    keyset = matmul(normed, image_attend[1]).astype(jnp.bfloat16).reshape(heads_shape)
    valueset = matmul(normed, image_attend[2]).astype(jnp.bfloat16).reshape(heads_shape)
    weights = softmax_last(
        contract("bqhd,bkhd->bhqk", queries, keyset) * HEAD_DIM ** (-0.5)
    ).astype(jnp.bfloat16)
    mixture = (
        contract("bhqk,bkhd->bqhd", weights, valueset)
        .astype(jnp.bfloat16)
        .reshape(group_size * length, model_width)
    )
    residual = flattened + matmul(mixture, image_output)
    normed_two = norm_rows(residual, image_gains[1], 0.0).astype(jnp.bfloat16)
    activated = jax.nn.gelu(matmul(normed_two, image_expand), approximate=True).astype(jnp.bfloat16)
    activated_mean = jnp.mean(
        activated.astype(jnp.float32).reshape(group_size, length, activated.shape[1]), axis=1
    )
    residual_mean = jnp.mean(residual.reshape(group_size, length, model_width), axis=1)
    pooled = residual_mean + matmul(activated_mean.astype(jnp.bfloat16), image_reduce)
    return unit_rows(pooled).astype(jnp.bfloat16)


def local(
    caption_tokens,
    image_tokens,
    image_attend,
    image_output,
    image_expand,
    image_reduce,
    image_gains,
    caption_attend,
    attend_bias,
    caption_output,
    output_bias,
    caption_expand,
    expand_bias,
    caption_reduce,
    reduce_bias,
    norm_gains,
    norm_shifts,
    log_scale,
    caption_image,
):
    local_embed = image_block(
        image_tokens, image_attend, image_output, image_expand, image_reduce, image_gains
    )
    group_images = lax.all_gather(local_embed, "mp", axis=0, tiled=True)
    captions, length, model_width = caption_tokens.shape
    row_count = captions * length
    heads_local = caption_attend.shape[2] // HEAD_DIM
    head_scale = HEAD_DIM ** (-0.5)

    def split_heads(matrix):
        return matrix.reshape(captions, length, heads_local, HEAD_DIM)

    flattened = caption_tokens.astype(jnp.float32).reshape(row_count, model_width)
    normed, norm_back_one = jax.vjp(norm_rows, flattened, norm_gains[0], norm_shifts[0])
    normed_low = normed.astype(jnp.bfloat16)
    queries = (matmul(normed_low, caption_attend[0]) + attend_bias[0]).astype(jnp.bfloat16)
    keyset = matmul(normed_low, caption_attend[1]).astype(jnp.bfloat16)
    valueset = (matmul(normed_low, caption_attend[2]) + attend_bias[1]).astype(jnp.bfloat16)
    weights = softmax_last(
        contract("bqhd,bkhd->bhqk", split_heads(queries), split_heads(keyset)) * head_scale
    )
    weights_low = weights.astype(jnp.bfloat16)
    mixture = (
        contract("bhqk,bkhd->bqhd", weights_low, split_heads(valueset))
        .astype(jnp.bfloat16)
        .reshape(row_count, heads_local * HEAD_DIM)
    )
    attended = lax.psum(matmul(mixture, caption_output).astype(jnp.bfloat16), "mp").astype(
        jnp.float32
    )
    residual = flattened + (attended + output_bias)
    normed_two, norm_back_two = jax.vjp(norm_rows, residual, norm_gains[1], norm_shifts[1])
    normed_two_low = normed_two.astype(jnp.bfloat16)
    hidden = matmul(normed_two_low, caption_expand) + expand_bias
    activated, activation_back = jax.vjp(partial(jax.nn.gelu, approximate=True), hidden)
    activated_low = activated.astype(jnp.bfloat16)
    activated_mean = jnp.mean(
        activated_low.astype(jnp.float32).reshape(captions, length, activated.shape[1]), axis=1
    ).astype(jnp.bfloat16)
    reduced = lax.psum(matmul(activated_mean, caption_reduce).astype(jnp.bfloat16), "mp").astype(
        jnp.float32
    )
    pooled = jnp.mean(residual.reshape(captions, length, model_width), axis=1) + (
        reduced + reduce_bias
    )
    embed, unit_back = jax.vjp(unit_rows, pooled)
    embed_low = embed.astype(jnp.bfloat16)
    scaling = jnp.exp(log_scale[0])
    devices_data = lax.axis_size("dp")
    total_captions = captions * devices_data
    total_images = group_images.shape[0] * devices_data
    portion = lax.all_gather(group_images, "dp", axis=0, tiled=True)
    row_top = jnp.full((captions,), -1e30, jnp.float32)
    portion_rows = portion.shape[0]
    scores = scaling * contract_last(embed_low, portion)
    matches = (caption_image[:, None] == lax.iota(jnp.int32, portion_rows)[None, :]).astype(
        jnp.float32
    )
    new_top = jnp.maximum(row_top, jnp.max(scores, axis=1))
    row_total = jnp.sum(jnp.exp(scores - new_top[:, None]), axis=1)
    row_positive = jnp.sum(scores * matches, axis=1)
    portion_top = jnp.max(scores, axis=0)
    column_top = portion_top
    column_total = jnp.sum(jnp.exp(scores - portion_top[None, :]), axis=0)
    column_positive = jnp.sum(scores * matches, axis=0)
    column_count = jnp.sum(matches, axis=0)
    everything = lax.all_gather(
        jnp.stack([column_top, column_total, column_positive, column_count]), "dp"
    )
    column_top = jnp.max(everything[:, 0], axis=0)
    column_total = jnp.sum(everything[:, 1] * jnp.exp(everything[:, 0] - column_top[None]), axis=0)
    column_positive = jnp.sum(everything[:, 2], axis=0)
    column_count = jnp.sum(everything[:, 3], axis=0)
    statistics = (new_top, row_total, row_positive)
    row_lse = statistics[0] + jnp.log(statistics[1])
    column_lse = column_top + jnp.log(column_total)
    column_inverse = 1.0 / column_count
    row_part = jnp.sum(row_lse - statistics[2])
    column_part = jnp.sum(column_lse - column_positive / column_count)
    image_weight = 0.5 * total_captions / total_images
    grad_scores = 0.5 * (jnp.exp(scores - row_lse[:, None]) - matches) + image_weight * (
        jnp.exp(scores - column_lse[None, :]) - matches * column_inverse[None, :]
    )
    grad_scale = jnp.sum(grad_scores * scores)
    grad_cosine = (scaling * grad_scores).astype(jnp.bfloat16)
    grad_embed = matmul(grad_cosine, portion)
    grad_pooled = unit_back(grad_embed)[0]
    grad_rows = jnp.broadcast_to(
        grad_pooled[:, None, :] * (1.0 / length), (captions, length, model_width)
    ).reshape(row_count, model_width)
    gradient_reduce_bias = jnp.sum(grad_pooled, axis=0)
    grad_pooled_low = grad_pooled.astype(jnp.bfloat16)
    gradient_reduce = outer_sum(activated_mean, grad_pooled_low)
    grad_activated = jnp.broadcast_to(
        (contract_last(grad_pooled_low, caption_reduce) * (1.0 / length))[:, None, :],
        (captions, length, caption_reduce.shape[0]),
    ).reshape(row_count, caption_reduce.shape[0])
    grad_hidden = activation_back(grad_activated)[0].astype(jnp.bfloat16)
    gradient_expand_bias = jnp.sum(grad_hidden.astype(jnp.float32), axis=0)
    gradient_expand = outer_sum(normed_two_low, grad_hidden)
    grad_normed_two = lax.psum(
        contract_last(grad_hidden, caption_expand).astype(jnp.bfloat16), "mp"
    ).astype(jnp.float32)
    grad_from_norm, gain_second, shift_second = norm_back_two(grad_normed_two)
    grad_residual = grad_rows + grad_from_norm
    grad_residual_low = grad_residual.astype(jnp.bfloat16)
    gradient_output_bias = jnp.sum(grad_residual, axis=0)
    gradient_output = outer_sum(mixture, grad_residual_low)
    grad_mixture = split_heads(
        contract_last(grad_residual_low, caption_output).astype(jnp.bfloat16)
    )
    grad_probs = contract("bqhd,bkhd->bhqk", grad_mixture, split_heads(valueset))
    grad_valueset = (
        contract("bhqk,bqhd->bkhd", weights_low, grad_mixture)
        .astype(jnp.bfloat16)
        .reshape(row_count, heads_local * HEAD_DIM)
    )
    grad_logits = (
        weights * (grad_probs - jnp.sum(grad_probs * weights, axis=-1, keepdims=True))
    ).astype(jnp.bfloat16)
    grad_queries = (
        (contract("bhqk,bkhd->bqhd", grad_logits, split_heads(keyset)) * head_scale)
        .astype(jnp.bfloat16)
        .reshape(row_count, heads_local * HEAD_DIM)
    )
    grad_keyset = (
        (contract("bhqk,bqhd->bkhd", grad_logits, split_heads(queries)) * head_scale)
        .astype(jnp.bfloat16)
        .reshape(row_count, heads_local * HEAD_DIM)
    )
    gradient_attend = jnp.stack(
        [
            outer_sum(normed_low, grad_queries),
            outer_sum(normed_low, grad_keyset),
            outer_sum(normed_low, grad_valueset),
        ]
    )
    gradient_attend_bias = jnp.stack(
        [
            jnp.sum(grad_queries.astype(jnp.float32), axis=0),
            jnp.sum(grad_valueset.astype(jnp.float32), axis=0),
        ]
    )
    partial_normed = (
        contract_last(grad_queries, caption_attend[0])
        + contract_last(grad_keyset, caption_attend[1])
        + contract_last(grad_valueset, caption_attend[2])
    )
    grad_normed = lax.psum(partial_normed.astype(jnp.bfloat16), "mp").astype(jnp.float32)
    grad_from_first, gain_first, shift_first = norm_back_one(grad_normed)
    gradient_tokens = (grad_residual + grad_from_first).reshape(captions, length, model_width)
    large = lax.psum(
        [
            part.astype(jnp.bfloat16)
            for part in (gradient_attend, gradient_output, gradient_expand, gradient_reduce)
        ],
        "dp",
    )
    large = [part.astype(jnp.float32) for part in large]
    small = lax.psum(
        (
            gradient_attend_bias,
            gradient_output_bias,
            gradient_expand_bias,
            gradient_reduce_bias,
            jnp.stack([gain_first, gain_second]),
            jnp.stack([shift_first, shift_second]),
            grad_scale,
            row_part,
        ),
        "dp",
    )
    summed = (
        large[0],
        small[0],
        large[1],
        small[1],
        large[2],
        small[2],
        large[3],
        small[3],
        small[4],
        small[5],
        small[6],
        small[7],
    )
    contrast_loss = (0.5 * (summed[11] / total_captions + column_part / total_images)).reshape(1)
    return (
        contrast_loss,
        gradient_tokens,
        summed[0],
        summed[1],
        summed[2],
        summed[3],
        summed[4],
        summed[5],
        summed[6],
        summed[7],
        summed[8],
        summed[9],
        summed[10].reshape(1),
    )


def solution(mesh):
    in_specs = (
        P("dp", None, None),
        P(("dp", "mp"), None, None),
        P(),
        P(),
        P(),
        P(),
        P(),
        P(None, None, "mp"),
        P(None, "mp"),
        P("mp", None),
        P(),
        P(None, "mp"),
        P("mp"),
        P("mp", None),
        P(),
        P(),
        P(),
        P(),
        P("dp"),
    )
    out_specs = (
        P(),
        P("dp", None, None),
        P(None, None, "mp"),
        P(None, "mp"),
        P("mp", None),
        P(),
        P(None, "mp"),
        P("mp"),
        P("mp", None),
        P(),
        P(),
        P(),
        P(),
    )
    return jax.shard_map(local, mesh=mesh, in_specs=in_specs, out_specs=out_specs, check_vma=False)
```

profile of v0, /device:TPU:0, one launch (start us, length us, event | category | flops | bytes accessed | tf_op | source)
XLA Modules:
  0.0 598.3 jit_solution(6334393651033239990)
XLA Ops:
  27.7 9.3 %fusion.131 = (f32[98,3,16]{2,1,0:T(4,128)S(1)}, f32[98,3,16,16]{2,3,1,0:T(8,128)S(1)}) fusion(f32[98,3,16,16]{2,3,1,0:T(8,128)S(1)} %fusion.66), kind=kOutput, calls=%fused_computation.244 | output fusion | flops 301071 | bytes 620928 | tf_op jit(solution)/shard_map/sub | solution.py:18
  40.6 4.0 reshape.460
  44.6 3.6 convolution_convert_fusion.1
  71.0 4.0 fusion.129
  82.8 3.2 fusion.130
  89.9 7.3 %fusion.32 = f32[350,3072]{1,0:T(8,128)} fusion(bf16[768,3072]{1,0:T(8,128)(2,1)} %param.23, f32[350,768]{1,0:T(8,128)} %get-tuple-element.71, f32[768]{0:T(1024)S(1)} %get-tuple-element.33, f32[350]{0:T(512)S(1)} %add_rsqrt_fusion.1, f32[350]{0:T(512)S(1)} %broadcast_multiply_fusion.4), kind=kOutput, calls=%fused_computation.72 | convolution fusion | flops 1663334400 | bytes 10100464 | tf_op jit(solution)/shard_map/dot_general | solution.py:27
  97.2 4.6 reshape.488
  103.2 3.0 reduce_sum.428
  106.2 3.3 multiply_reduce_fusion.10
  109.6 38.7 %all-reduce.8.cloned.1.call-done = bf16[1568,768]{1,0:T(8,128)(2,1)} async-done(((bf16[1568,768]{1,0:T(8,128)(2,1)}), bf16[1568,768]{1,0:T(8,128)(2,1)}) %all-reduce.8.cloned.1.call-update) | async-done | bytes 2408464 | tf_op jit(solution)/shard_map/psum | solution.py:122
  148.3 5.2 add_add_fusion.3
  156.3 3.2 multiply_reduce_fusion
  161.2 5.1 multiply_convert_fusion
  169.8 13.3 %all-gather.1 = bf16[4,7,768]{2,1,0:T(8,128)(2,1)S(1)} all-gather(bf16[1,7,768]{2,1,0:T(8,128)(2,1)S(1)} %fusion.108), channel_id=1, replica_groups=mesh['dp'=8,'mp'=4] {'mp'}, dimensions={0}, use_global_device_ids=true | all-gather | bytes 53760 | tf_op jit(solution)/shard_map/all_gather | solution.py:98
  183.2 10.5 %all-gather.2 = bf16[8,28,768]{2,1,0:T(8,128)(2,1)} all-gather(bf16[1,28,768]{2,1,0:T(8,128)(2,1)S(1)} %reshape.492), channel_id=1, replica_groups=mesh['dp'=8,'mp'=4] {'dp'}, dimensions={0}, use_global_device_ids=true | all-gather | bytes 387072 | tf_op jit(solution)/shard_map/all_gather | solution.py:146
  194.8 3.2 reduce_sum.417
  198.0 4.8 all-reduce.10.cloned.1.call-done
  206.3 9.0 %all-gather.3 = f32[8,4,224]{2,1,0:T(4,128)S(1)} all-gather(f32[1,4,224]{2,1,0:T(4,128)S(1)} %maximum_bitcast_fusion), channel_id=2, replica_groups=mesh['dp'=8,'mp'=4] {'dp'}, dimensions={0}, use_global_device_ids=true | all-gather | bytes 32256 | tf_op jit(solution)/shard_map/all_gather | solution.py:161
  218.7 6.1 %convert_reduce_fusion.3 = (f32[768]{0:T(1024)}, bf16[1568,768]{1,0:T(8,128)(2,1)S(1)}) fusion(f32[1568,768]{1,0:T(8,128)} %get-tuple-element.77, f32[768]{0:T(1024)S(1)} %copy-done.64, f32[98,768]{1,0:T(8,128)S(1)} %convolution_multiply_fusion), kind=kLoop, calls=%fused_computation.35 | loop fusion | flops 27696384 | bytes 7532544 | tf_op jit(solution)/shard_map/reduce_sum | solution.py:193
  226.2 3.5 convolution_convert_fusion
  232.3 5.2 convolution_convert_fusion.8
  237.5 88.7 %all-reduce.12.cloned.1.call-done = bf16[1568,768]{1,0:T(8,128)(2,1)} async-done(((bf16[1568,768]{1,0:T(8,128)(2,1)}), bf16[1568,768]{1,0:T(8,128)(2,1)}) %all-reduce.12.cloned.1.call-update) | async-done | bytes 2408464 | tf_op jit(solution)/shard_map/psum | solution.py:195
  326.1 5.1 fusion.15
  331.3 4.1 fusion.126
  342.0 3.8 multiply_reduce_fusion.2
  357.8 3.0 reshape.476
  360.9 3.2 fusion.57
  381.0 65.3 %all-reduce.16.cloned.1.call-done = (bf16[3,768,192]{1,2,0:T(8,128)(2,1)}, bf16[192,768]{1,0:T(8,128)(2,1)}, bf16[768,768]{1,0:T(8,128)(2,1)}, bf16[768,768]{1,0:T(8,128)(2,1)}) async-done(((bf16[3,768,192]{1,2,0:T(8,128)(2,1)}, bf16[192,768]{1,0:T(8,128)(2,1)}, bf16[768,768]{1,0:T(8,128)(2,1)}, bf16[768,768]{1,0:T(8,128)(2,1)}), (bf16[3,768,192]{1,2,0:T(8,128)(2,1)}, bf16[192,768]{1,0:T(8,128)(2,1)}, ...) | async-done | bytes 3538960 | tf_op jit(solution)/shard_map/psum | solution.py:246
  454.0 92.7 %all-reduce.14.cloned.1.call-done = bf16[1568,768]{1,0:T(8,128)(2,1)} async-done(((bf16[1568,768]{1,0:T(8,128)(2,1)}), bf16[1568,768]{1,0:T(8,128)(2,1)}) %all-reduce.14.cloned.1.call-update) | async-done | bytes 2408464 | tf_op jit(solution)/shard_map/psum | solution.py:243
  546.7 5.4 fusion.16
  557.9 7.1 %add_add_fusion.2 = (f32[1568,768]{1,0:T(8,128)}, f32[768]{0:T(1024)S(1)}) fusion(f32[1568,768]{1,0:T(8,128)} %add_add_fusion, f32[1568,768]{1,0:T(8,128)} %copy-done.5, f32[1568]{0:T(1024)S(1)} %negate_multiply_fusion, f32[1568]{0:T(1024)S(1)} %negate_multiply_fusion.1, f32[98,768]{1,0:T(8,128)S(1)} %copy-done.18), kind=kLoop, calls=%fused_computation.36 | loop fusion | flops 6020352 | bytes 14767360 | tf_op jit(solution)/shard_map/add | solution.py:245
  565.0 24.6 %all-reduce = (f32[]{:T(128)}, f32[2,192]{1,0:T(2,128)}, f32[768]{0:T(1024)}, f32[768]{0:T(1024)}, f32[768]{0:T(1024)}, /*index=5*/f32[2,768]{1,0:T(2,128)}, f32[2,768]{1,0:T(2,128)}, f32[1]{0:T(128)}) all-reduce(f32[]{:T(128)} %subtract_reduce_fusion.1, f32[2,192]{1,0:T(2,128)S(1)} %pad_maximum_fusion.3, ...), channel_id=1, replica_groups=mesh['dp'=8,'mp'=4] {'dp'}, use_global_device_ids=true, to_apply=%region_24.0 | all-reduce | flops 5762 | bytes 46096 | tf_op jit(solution)/shard_map/psum | solution.py:254
  (258 shorter events, 126.8 us)
Async XLA Ops:
  7.2 154.0 %copy-start = (bf16[768,768]{1,0:T(8,128)(2,1)S(1)}, bf16[768,768]{1,0:T(8,128)(2,1)}, u32[]{:S(2)}) copy-start(bf16[768,768]{1,0:T(8,128)(2,1)} %param.30) | copy-start | bytes 3538948
  7.2 141.1 %all-reduce.8.cloned.1.call-start = ((), (), s32[]{:S(2)}) async-start(), calls=%async_computation | async-start | bytes 4816896 | tf_op jit(solution)/shard_map/psum | solution.py:122
  11.8 147.7 %copy-start.51 = (f32[768]{0:T(1024)}, f32[768]{0:T(1024)S(1)}, u32[]{:S(2)}) copy-start(f32[768]{0:T(1024)S(1)} %get-tuple-element.88) | copy-start | bytes 9220
  27.7 9.4 %copy-start.24 = (bf16[98,16,3,64]{3,2,1,0:T(4,128)(2,1)S(1)}, bf16[98,16,3,64]{3,2,1,0:T(4,128)(2,1)}, u32[]{:S(2)}) copy-start(bf16[98,16,3,64]{3,2,1,0:T(4,128)(2,1)} %reshape.457) | copy-start | bytes 1806340
  44.6 3.8 copy-start.10
  48.1 154.7 %all-reduce.10.cloned.1.call-start = ((), (), s32[]{:S(2)}) async-start(), calls=%async_computation.1 | async-start | bytes 319488 | tf_op jit(solution)/shard_map/psum | solution.py:134
  71.0 4.0 copy-start.26
  106.2 42.1 %copy-start.65 = (f32[768]{0:T(1024)S(1)}, f32[768]{0:T(1024)}, u32[]{:S(2)}) copy-start(f32[768]{0:T(1024)} %param.29) | copy-start | bytes 9220
  156.2 3.8 copy-start.2
  161.2 5.1 copy-start.23
  169.0 157.1 %all-reduce.12.cloned.1.call-start = ((), (), s32[]{:S(2)}) async-start(), calls=%async_computation.2 | async-start | bytes 4816896 | tf_op jit(solution)/shard_map/psum | solution.py:195
  194.8 8.0 %copy-start.49 = (f32[768]{0:T(1024)S(1)}, f32[768]{0:T(1024)}, u32[]{:S(2)}) copy-start(f32[768]{0:T(1024)} %param.33) | copy-start | bytes 9220
  202.8 14.6 %copy-start.19 = (bf16[98,768]{1,0:T(8,128)(2,1)S(1)}, bf16[98,768]{1,0:T(8,128)(2,1)}, u32[]{:S(2)}) copy-start(bf16[98,768]{1,0:T(8,128)(2,1)} %all-reduce.10.cloned.1.call-done) | copy-start | bytes 451588
  202.8 14.6 %copy-start.50 = (f32[768]{0:T(1024)S(1)}, f32[768]{0:T(1024)}, u32[]{:S(2)}) copy-start(f32[768]{0:T(1024)} %param.33) | copy-start | bytes 9220
  202.8 15.3 %copy-start.13 = (bf16[768,768]{1,0:T(8,128)(2,1)S(1)}, bf16[768,768]{1,0:T(8,128)(2,1)}, u32[]{:S(2)}) copy-start(bf16[768,768]{1,0:T(8,128)(2,1)} %param.32) | copy-start | bytes 3538948
  205.3 13.3 %copy-start.64 = (f32[768]{0:T(1024)S(1)}, f32[768]{0:T(1024)}, u32[]{:S(2)}) copy-start(f32[768]{0:T(1024)} %param.31) | copy-start | bytes 9220
  206.3 11.9 %copy-start.66 = (f32[98]{0:T(128)}, f32[98]{0:T(128)S(1)}, u32[]{:S(2)}) copy-start(f32[98]{0:T(128)S(1)} %log_add_fusion.1) | copy-start | bytes 1180
  229.8 216.5 %all-reduce.16.cloned.1.call-start = ((), (), s32[]{:S(2)}) async-start(), calls=%async_computation.4 | async-start | bytes 7077888 | tf_op jit(solution)/shard_map/psum | solution.py:246
  230.7 104.7 %copy-start.17 = (f32[98,768]{1,0:T(8,128)}, f32[98,768]{1,0:T(8,128)S(1)}, u32[]{:S(2)}) copy-start(f32[98,768]{1,0:T(8,128)S(1)} %broadcast_multiply_fusion) | copy-start | bytes 903172
  232.3 93.9 %copy-start.42 = (f32[1568]{0:T(1024)S(1)}, f32[1568]{0:T(1024)}, u32[]{:S(2)}) copy-start(f32[1568]{0:T(1024)} %copy-done.41) | copy-start | bytes 18820
  232.3 93.9 %copy-start.44 = (f32[1568]{0:T(1024)S(1)}, f32[1568]{0:T(1024)}, u32[]{:S(2)}) copy-start(f32[1568]{0:T(1024)} %copy-done.43) | copy-start | bytes 18820
  232.3 93.9 %copy-start.52 = (f32[768]{0:T(1024)S(1)}, f32[768]{0:T(1024)}, u32[]{:S(2)}) copy-start(f32[768]{0:T(1024)} %copy-done.51) | copy-start | bytes 9220
  237.4 93.8 %copy-start.46 = (f32[1568]{0:T(1024)S(1)}, f32[1568]{0:T(1024)}, u32[]{:S(2)}) copy-start(f32[1568]{0:T(1024)} %copy-done.45) | copy-start | bytes 18820
  326.1 5.1 copy-start.9
  372.7 174.0 %all-reduce.14.cloned.1.call-start = ((), (), s32[]{:S(2)}) async-start(), calls=%async_computation.3 | async-start | bytes 4816896 | tf_op jit(solution)/shard_map/psum | solution.py:243
  446.3 4.4 copy-start.30
  452.3 94.3 %copy-start.48 = (f32[768]{0:T(1024)S(1)}, f32[768]{0:T(1024)}, u32[]{:S(2)}) copy-start(f32[768]{0:T(1024)} %copy-done.47) | copy-start | bytes 9220
  546.7 5.4 copy-start.4
  546.7 5.4 copy-start.6
  557.9 7.2 %copy-start.53 = (f32[768]{0:T(1024)S(1)}, f32[768]{0:T(1024)}, u32[]{:S(2)}) copy-start(f32[768]{0:T(1024)} %get-tuple-element.52) | copy-start | bytes 9220
  557.9 7.2 %copy-start.54 = (f32[768]{0:T(1024)S(1)}, f32[768]{0:T(1024)}, u32[]{:S(2)}) copy-start(f32[768]{0:T(1024)} %get-tuple-element.50) | copy-start | bytes 9220
  557.9 32.4 %copy-start.1 = (bf16[768,768]{1,0:T(8,128)(2,1)S(1)}, bf16[768,768]{1,0:T(8,128)(2,1)}, u32[]{:S(2)}) copy-start(bf16[768,768]{1,0:T(8,128)(2,1)} %param.30) | copy-start | bytes 3538948
  (41 other events, 81.1 us)
Sparse Core Ops, SparseCore 0:
  48.3 100.0 all-reduce.7
  169.1 33.5 all-reduce.9
  229.9 96.1 all-reduce.11
  372.8 73.4 all-reduce.15
  449.3 97.3 all-reduce.13
where the time goes:
time: 607 us; the launch traced here: 598 us
  waiting for transfers between devices  290 us (48%)
  other arithmetic  90.2 us (15%)
  matrix products  80.7 us (13%)
  local copies, waits for them, and re-layouts  60.7 us (10%)
  blocking collectives  57.5 us (9%)
  between operations  18.3 us (3%)
    psum x1, waiting for transfers between devices, local(): lax.psum(partial_normed.astype(jnp.bfloat16), 'mp').astype(jnp.float32)  92.7 us
    psum x1, waiting for transfers between devices, local(): lax.psum(contract_last(grad_hidden, caption_expand).astype(jnp.bfloat16),...  88.7 us
    psum x1, waiting for transfers between devices, local(): lax.psum([part.astype(jnp.bfloat16) for part in (gradient_attend, gradien...  65.3 us
    psum x1, waiting for transfers between devices, local(): lax.psum(matmul(mixture, caption_output).astype(jnp.bfloat16), 'mp')  38.7 us
    dot_general x13, matrix products, matmul(): return jnp.dot(left_side, right_side, preferred_element_type=jnp.float32)  37.7 us
    psum x1, blocking collectives, local(): lax.psum((gradient_attend_bias, gradient_output_bias, gradient_expand_bia...  24.6 us
    dot_general x6, matrix products, outer_sum(): lax.dot_general(left_side, right_side, (((0,), (0,)), ((), ())), preferre...  16.4 us
    dot_general x8, matrix products, contract(): jnp.einsum(formula, left_side, right_side, preferred_element_type=jnp.flo...  15.5 us
  transfers between devices with their start and end apart: 5, of which 5 were waited for; matrix products, arithmetic and copies ran while one was open for 14% of the time, Pallas kernels for 0%

commit v1 on v0

--- a/solution.py
+++ b/solution.py
@@ -119,9 +119,9 @@
         .astype(jnp.bfloat16)
         .reshape(row_count, heads_local * HEAD_DIM)
     )
-    attended = lax.psum(matmul(mixture, caption_output).astype(jnp.bfloat16), "mp").astype(
-        jnp.float32
-    )
+    attended = jnp.sum(
+        lax.all_gather(matmul(mixture, caption_output).astype(jnp.bfloat16), "mp"), axis=0
+    ).astype(jnp.float32)
     residual = flattened + (attended + output_bias)
     normed_two, norm_back_two = jax.vjp(norm_rows, residual, norm_gains[1], norm_shifts[1])
     normed_two_low = normed_two.astype(jnp.bfloat16)

time: 607 us -> 688 us (1.13)
  waiting for transfers between devices: 290 us -> 368 us
    all_gather x0 -> x1, waiting for transfers between devices: none -> 115 us  [local(): lax.all_gather(matmul(mixture, caption_output).astype(jnp.bfloat16), 'mp')]
    psum x1 -> x0, waiting for transfers between devices: 38.7 us -> none  [local(): lax.psum(matmul(mixture, caption_output).astype(jnp.bfloat16), 'mp')]
    reduce_sum x0 -> x1, other arithmetic: none -> 7.23 us  [local(): jnp.sum(lax.all_gather(matmul(mixture, caption_output).astype(jnp.bfloat1...]
  transfers between devices with their start and end apart: 5 -> 5, of which waited for: 5 -> 5; matrix products, arithmetic and copies ran while one was open for 14% -> 12% of each run, Pallas kernels for 0% -> 0%
where the time goes in v1:
time: 688 us; the launch traced here: 680 us
  waiting for transfers between devices  368 us (53%)
  other arithmetic  95.8 us (14%)
  matrix products  81 us (12%)
  local copies, waits for them, and re-layouts  58 us (8%)
  blocking collectives  57.5 us (8%)
  between operations  18.4 us (3%)
    all_gather x1, waiting for transfers between devices, local(): lax.all_gather(matmul(mixture, caption_output).astype(jnp.bfloat16), 'mp')  115 us
    psum x1, waiting for transfers between devices, local(): lax.psum(partial_normed.astype(jnp.bfloat16), 'mp').astype(jnp.float32)  92.5 us
    psum x1, waiting for transfers between devices, local(): lax.psum(contract_last(grad_hidden, caption_expand).astype(jnp.bfloat16),...  88.7 us
    psum x1, waiting for transfers between devices, local(): lax.psum([part.astype(jnp.bfloat16) for part in (gradient_attend, gradien...  65.1 us
    dot_general x13, matrix products, matmul(): return jnp.dot(left_side, right_side, preferred_element_type=jnp.float32)  37.6 us
    psum x1, blocking collectives, local(): lax.psum((gradient_attend_bias, gradient_output_bias, gradient_expand_bia...  24.6 us
    dot_general x6, matrix products, outer_sum(): lax.dot_general(left_side, right_side, (((0,), (0,)), ((), ())), preferre...  16.4 us
    dot_general x8, matrix products, contract(): jnp.einsum(formula, left_side, right_side, preferred_element_type=jnp.flo...  14.4 us
  transfers between devices with their start and end apart: 5, of which 5 were waited for; matrix products, arithmetic and copies ran while one was open for 12% of the time, Pallas kernels for 0%

profile of v1, /device:TPU:0, one launch (start us, length us, event | category | flops | bytes accessed | tf_op | source)
XLA Modules:
  0.0 679.9 jit_solution(5772658626001903689)
XLA Ops:
  27.6 9.3 %fusion.132 = (f32[98,3,16]{2,1,0:T(4,128)S(1)}, f32[98,3,16,16]{2,3,1,0:T(8,128)S(1)}) fusion(f32[98,3,16,16]{2,3,1,0:T(8,128)S(1)} %fusion.68), kind=kOutput, calls=%fused_computation.247 | output fusion | flops 301071 | bytes 620928 | tf_op jit(solution)/shard_map/sub | solution.py:18
  40.5 4.0 reshape.494
  44.5 3.5 convolution_convert_fusion.1
  71.2 4.0 fusion.130
  79.6 3.2 fusion.131
  86.7 7.5 %fusion.32 = f32[350,3072]{1,0:T(8,128)} fusion(bf16[768,3072]{1,0:T(8,128)(2,1)} %param.23, f32[350,768]{1,0:T(8,128)} %get-tuple-element.76, f32[768]{0:T(1024)S(1)} %get-tuple-element.35, f32[350]{0:T(512)S(1)} %add_rsqrt_fusion.1, f32[350]{0:T(512)S(1)} %broadcast_multiply_fusion.4), kind=kOutput, calls=%fused_computation.74 | convolution fusion | flops 1663334400 | bytes 10100464 | tf_op jit(solution)/shard_map/dot_general | solution.py:27
  94.1 4.6 reshape.523
  103.0 3.2 multiply_reduce_fusion.10
  106.2 114.6 %all-gather.7.cloned.1.call-done = bf16[6272,768]{1,0:T(8,128)(2,1)} async-done(((bf16[1568,768]{1,0:T(8,128)(2,1)}), bf16[6272,768]{1,0:T(8,128)(2,1)}) %all-gather.7.cloned.1.call-update) | async-done | bytes 9633808 | tf_op jit(solution)/shard_map/all_gather | solution.py:123
  220.8 7.2 %reduce_sum.429 = bf16[1568,768]{1,0:T(8,128)(2,1)} reduce(bf16[4,1568,768]{2,1,0:T(8,128)(2,1)} %bitcast.139, bf16[]{:T(256)} %constant.27.clone.1), dimensions={0}, to_apply=%region_4.0 | reduce | flops 3612672 | bytes 12042242 | tf_op jit(solution)/shard_map/reduce_sum | solution.py:122
  228.0 6.0 fusion.45
  234.2 4.2 multiply_reduce_fusion
  238.6 4.6 add_convert_fusion.1
  243.2 5.1 multiply_convert_fusion
  251.9 13.1 %all-gather.2 = bf16[4,7,768]{2,1,0:T(8,128)(2,1)S(1)} all-gather(bf16[1,7,768]{2,1,0:T(8,128)(2,1)S(1)} %fusion.110), channel_id=1, replica_groups=mesh['dp'=8,'mp'=4] {'mp'}, dimensions={0}, use_global_device_ids=true | all-gather | bytes 53760 | tf_op jit(solution)/shard_map/all_gather | solution.py:98
  265.0 10.8 %all-gather.3 = bf16[8,28,768]{2,1,0:T(8,128)(2,1)} all-gather(bf16[1,28,768]{2,1,0:T(8,128)(2,1)S(1)} %reshape.528), channel_id=1, replica_groups=mesh['dp'=8,'mp'=4] {'dp'}, dimensions={0}, use_global_device_ids=true | all-gather | bytes 387072 | tf_op jit(solution)/shard_map/all_gather | solution.py:146
  276.8 7.1 %all-reduce.7.cloned.1.call-done = bf16[98,768]{1,0:T(8,128)(2,1)} async-done(((bf16[98,768]{1,0:T(8,128)(2,1)}), bf16[98,768]{1,0:T(8,128)(2,1)}) %all-reduce.7.cloned.1.call-update) | async-done | bytes 150544 | tf_op jit(solution)/shard_map/psum | solution.py:134
  287.6 9.0 %all-gather.4 = f32[8,4,224]{2,1,0:T(4,128)S(1)} all-gather(f32[1,4,224]{2,1,0:T(4,128)S(1)} %maximum_bitcast_fusion), channel_id=3, replica_groups=mesh['dp'=8,'mp'=4] {'dp'}, dimensions={0}, use_global_device_ids=true | all-gather | bytes 32256 | tf_op jit(solution)/shard_map/all_gather | solution.py:161
  302.0 4.2 convert_reduce_fusion.3
  307.7 3.5 convolution_convert_fusion
  313.8 5.2 convolution_convert_fusion.8
  318.9 88.7 %all-reduce.9.cloned.1.call-done = bf16[1568,768]{1,0:T(8,128)(2,1)} async-done(((bf16[1568,768]{1,0:T(8,128)(2,1)}), bf16[1568,768]{1,0:T(8,128)(2,1)}) %all-reduce.9.cloned.1.call-update) | async-done | bytes 2408464 | tf_op jit(solution)/shard_map/psum | solution.py:195
  407.7 5.1 fusion.15
  412.8 4.1 fusion.127
  423.5 3.8 multiply_reduce_fusion.2
  439.4 3.0 reshape.510
  442.4 3.2 fusion.59
  462.8 65.1 %all-reduce.13.cloned.1.call-done = (bf16[3,768,192]{1,2,0:T(8,128)(2,1)}, bf16[192,768]{1,0:T(8,128)(2,1)}, bf16[768,768]{1,0:T(8,128)(2,1)}, bf16[768,768]{1,0:T(8,128)(2,1)}) async-done(((bf16[3,768,192]{1,2,0:T(8,128)(2,1)}, bf16[192,768]{1,0:T(8,128)(2,1)}, bf16[768,768]{1,0:T(8,128)(2,1)}, bf16[768,768]{1,0:T(8,128)(2,1)}), (bf16[3,768,192]{1,2,0:T(8,128)(2,1)}, bf16[192,768]{1,0:T(8,128)(2,1)}, ...) | async-done | bytes 3538960 | tf_op jit(solution)/shard_map/psum | solution.py:246
  535.6 92.5 %all-reduce.11.cloned.1.call-done = bf16[1568,768]{1,0:T(8,128)(2,1)} async-done(((bf16[1568,768]{1,0:T(8,128)(2,1)}), bf16[1568,768]{1,0:T(8,128)(2,1)}) %all-reduce.11.cloned.1.call-update) | async-done | bytes 2408464 | tf_op jit(solution)/shard_map/psum | solution.py:243
  628.1 5.4 fusion.16
  639.3 7.1 %add_add_fusion.2 = (f32[1568,768]{1,0:T(8,128)}, f32[768]{0:T(1024)S(1)}) fusion(f32[1568,768]{1,0:T(8,128)} %add_add_fusion, f32[1568,768]{1,0:T(8,128)} %copy-done.4, f32[1568]{0:T(1024)S(1)} %negate_multiply_fusion, f32[1568]{0:T(1024)S(1)} %negate_multiply_fusion.1, f32[98,768]{1,0:T(8,128)S(1)} %copy-done.17), kind=kLoop, calls=%fused_computation.37 | loop fusion | flops 6020352 | bytes 14767360 | tf_op jit(solution)/shard_map/add | solution.py:245
  646.5 24.6 %all-reduce = (f32[]{:T(128)}, f32[2,192]{1,0:T(2,128)}, f32[768]{0:T(1024)}, f32[768]{0:T(1024)}, f32[768]{0:T(1024)}, /*index=5*/f32[2,768]{1,0:T(2,128)}, f32[2,768]{1,0:T(2,128)}, f32[1]{0:T(128)}) all-reduce(f32[]{:T(128)} %subtract_reduce_fusion.1, f32[2,192]{1,0:T(2,128)S(1)} %pad_maximum_fusion.3, ...), channel_id=1, replica_groups=mesh['dp'=8,'mp'=4] {'dp'}, use_global_device_ids=true, to_apply=%region_24.0 | all-reduce | flops 5762 | bytes 46096 | tf_op jit(solution)/shard_map/psum | solution.py:254
  (254 shorter events, 124.7 us)
Async XLA Ops:
  7.2 236.0 %copy-start = (bf16[768,768]{1,0:T(8,128)(2,1)S(1)}, bf16[768,768]{1,0:T(8,128)(2,1)}, u32[]{:S(2)}) copy-start(bf16[768,768]{1,0:T(8,128)(2,1)} %param.30) | copy-start | bytes 3538948
  7.2 213.6 %all-gather.7.cloned.1.call-start = ((), (), s32[]{:S(2)}) async-start(), calls=%async_computation.3 | async-start | bytes 12042240 | tf_op jit(solution)/shard_map/all_gather | solution.py:123
  11.8 226.8 %copy-start.48 = (f32[768]{0:T(1024)}, f32[768]{0:T(1024)S(1)}, u32[]{:S(2)}) copy-start(f32[768]{0:T(1024)S(1)} %get-tuple-element.93) | copy-start | bytes 9220
  27.6 9.4 %copy-start.23 = (bf16[98,16,3,64]{3,2,1,0:T(4,128)(2,1)S(1)}, bf16[98,16,3,64]{3,2,1,0:T(4,128)(2,1)}, u32[]{:S(2)}) copy-start(bf16[98,16,3,64]{3,2,1,0:T(4,128)(2,1)} %reshape.491) | copy-start | bytes 1806340
  48.0 236.0 %all-reduce.7.cloned.1.call-start = ((), (), s32[]{:S(2)}) async-start(), calls=%async_computation | async-start | bytes 319488 | tf_op jit(solution)/shard_map/psum | solution.py:134
  220.8 7.2 %copy-start.50 = (f32[768]{0:T(1024)S(1)}, f32[768]{0:T(1024)}, u32[]{:S(2)}) copy-start(f32[768]{0:T(1024)} %param.29) | copy-start | bytes 9220
  234.2 4.4 copy-start.39
  238.5 4.7 copy-start.43
  238.5 4.7 copy-start.41
  238.5 4.7 copy-start.61
  243.2 5.1 copy-start.22
  248.3 35.7 %copy-start.47 = (f32[768]{0:T(1024)S(1)}, f32[768]{0:T(1024)}, u32[]{:S(2)}) copy-start(f32[768]{0:T(1024)} %param.33) | copy-start | bytes 9220
  251.0 156.6 %all-reduce.9.cloned.1.call-start = ((), (), s32[]{:S(2)}) async-start(), calls=%async_computation.1 | async-start | bytes 4816896 | tf_op jit(solution)/shard_map/psum | solution.py:195
  284.0 14.8 %copy-start.18 = (bf16[98,768]{1,0:T(8,128)(2,1)S(1)}, bf16[98,768]{1,0:T(8,128)(2,1)}, u32[]{:S(2)}) copy-start(bf16[98,768]{1,0:T(8,128)(2,1)} %all-reduce.7.cloned.1.call-done) | copy-start | bytes 451588
  285.1 16.9 %copy-start.11 = (f32[1568,768]{1,0:T(8,128)S(1)}, f32[1568,768]{1,0:T(8,128)}, u32[]{:S(2)}) copy-start(f32[1568,768]{1,0:T(8,128)} %get-tuple-element.82) | copy-start | bytes 14450692
  286.6 15.4 %copy-start.62 = (f32[768]{0:T(1024)S(1)}, f32[768]{0:T(1024)}, u32[]{:S(2)}) copy-start(f32[768]{0:T(1024)} %param.31) | copy-start | bytes 9220
  287.6 14.4 %copy-start.63 = (f32[98]{0:T(128)}, f32[98]{0:T(128)S(1)}, u32[]{:S(2)}) copy-start(f32[98]{0:T(128)S(1)} %log_add_fusion.1) | copy-start | bytes 1180
  311.3 216.6 %all-reduce.13.cloned.1.call-start = ((), (), s32[]{:S(2)}) async-start(), calls=%async_computation.4 | async-start | bytes 7077888 | tf_op jit(solution)/shard_map/psum | solution.py:246
  312.3 104.7 %copy-start.16 = (f32[98,768]{1,0:T(8,128)}, f32[98,768]{1,0:T(8,128)S(1)}, u32[]{:S(2)}) copy-start(f32[98,768]{1,0:T(8,128)S(1)} %broadcast_multiply_fusion) | copy-start | bytes 903172
  313.8 93.9 %copy-start.40 = (f32[1568]{0:T(1024)S(1)}, f32[1568]{0:T(1024)}, u32[]{:S(2)}) copy-start(f32[1568]{0:T(1024)} %copy-done.39) | copy-start | bytes 18820
  313.8 93.9 %copy-start.42 = (f32[1568]{0:T(1024)S(1)}, f32[1568]{0:T(1024)}, u32[]{:S(2)}) copy-start(f32[1568]{0:T(1024)} %copy-done.41) | copy-start | bytes 18820
  313.8 93.9 %copy-start.49 = (f32[768]{0:T(1024)S(1)}, f32[768]{0:T(1024)}, u32[]{:S(2)}) copy-start(f32[768]{0:T(1024)} %copy-done.48) | copy-start | bytes 9220
  407.7 5.1 copy-start.44
  407.7 5.1 copy-start.8
  454.3 173.8 %all-reduce.11.cloned.1.call-start = ((), (), s32[]{:S(2)}) async-start(), calls=%async_computation.2 | async-start | bytes 4816896 | tf_op jit(solution)/shard_map/psum | solution.py:243
  527.9 4.4 copy-start.29
  533.9 94.2 %copy-start.46 = (f32[768]{0:T(1024)S(1)}, f32[768]{0:T(1024)}, u32[]{:S(2)}) copy-start(f32[768]{0:T(1024)} %copy-done.45) | copy-start | bytes 9220
  628.1 5.4 copy-start.3
  628.1 5.4 copy-start.5
  639.3 7.2 %copy-start.51 = (f32[768]{0:T(1024)S(1)}, f32[768]{0:T(1024)}, u32[]{:S(2)}) copy-start(f32[768]{0:T(1024)} %get-tuple-element.54) | copy-start | bytes 9220
  639.3 7.2 %copy-start.52 = (f32[768]{0:T(1024)S(1)}, f32[768]{0:T(1024)}, u32[]{:S(2)}) copy-start(f32[768]{0:T(1024)} %get-tuple-element.52) | copy-start | bytes 9220
  639.3 32.4 %copy-start.1 = (bf16[768,768]{1,0:T(8,128)(2,1)S(1)}, bf16[768,768]{1,0:T(8,128)(2,1)}, u32[]{:S(2)}) copy-start(bf16[768,768]{1,0:T(8,128)(2,1)} %param.30) | copy-start | bytes 3538948
  (38 other events, 81.2 us)
Sparse Core Ops, SparseCore 0:
  48.1 172.6 all-gather.6
  251.2 32.7 all-reduce.6
  311.4 96.1 all-reduce.8
  454.4 73.4 all-reduce.12
  530.7 97.3 all-reduce.10
